TPU v7x, 128 devices: a whole 4x4x4 slice. The times are simulated.
128 devices in a mesh: goal: 8 (over z, core), cand: 16 (over x, y).
Axes of the slice: x: 4, y: 4, z: 4, core: 2. Of those that a mesh axis runs over, the one named last changes fastest.
Arguments:
- dec_states: bfloat16 [8, 32, 24, 4096], P('goal', 'cand'), may hold values from -18 to 18
- memory: bfloat16 [8, 512, 4096], P('goal', 'cand'), may hold values from -18 to 18
- counts: int32 [8], P('goal'), may hold values from 2 to 30, as said below
- rank: int32 [8, 32], P('goal'), may hold values from 0 to 31, each once within a row
- visits: int32 [8, 32], P('goal'), may hold values from 1 to 64
- w_query: bfloat16 [4096, 4096], P(None, 'cand'), may hold values from -1 to 1
- w_key: bfloat16 [4096, 4096], P(None, 'cand'), may hold values from -1 to 1
- w_value: bfloat16 [4096, 4096], P(None, 'cand'), may hold values from -0.3125 to 0.3125
- w_out: bfloat16 [4096, 4096], P('cand'), may hold values from -0.25 to 0.25
- gain: float32 [4096], replicated, may hold values from 0.5 to 1.5
- w_score: float32 [4096], replicated, may hold values from -0.5 to 0.5
Outputs:
- log_probs: float32 [8, 32], P('goal', 'cand')
- goal_loss: float32 [8], P('goal')
- grad_query: bfloat16 [4096, 4096], P('goal', 'cand')
- grad_key: bfloat16 [4096, 4096], P('goal', 'cand')
- grad_value: bfloat16 [4096, 4096], P('goal', 'cand')
- grad_out: bfloat16 [4096, 4096], P('cand', 'goal')
Inputs may be any that keep to these rules, and one draw needn't show every extreme that they name: `counts`: every goal has 2 to 30 candidates, and some goal has exactly 30. `rank`: each goal's row is a permutation; the slot holding candidate number j is live when j is below the goal's count.
All inputs are finite; a program needn't handle non-finite values.
Results may differ from a plain program's by a relative error of at most 0.015.
Values may be sent and summed in bfloat16 or wider, within the bound.
No kernel may reach another device: no remote copies, remote signals or barrier semaphores. Data moves between devices by JAX's collectives and lax.ppermute only.
A program may use at most 128 MiB of HBM per device.

v0:
```python
import jax
import jax.numpy as jnp
from jax import lax
from jax.sharding import PartitionSpec as P

HD = 64


def rounded(values):
    return lax.optimization_barrier(values.astype(jnp.bfloat16)).astype(jnp.float32)


def attend(query, key, value, heads_here):
    total_rows = query.shape[0]
    memory_rows = key.shape[0]
    query_heads = query.reshape(total_rows, heads_here, HD)
    key_heads = key.reshape(memory_rows, heads_here, HD)
    value_heads = value.reshape(memory_rows, heads_here, HD)
    scores = jnp.einsum(
        "rhe,mhe->hrm", query_heads, key_heads, preferred_element_type=jnp.float32
    ) * HD ** (-0.5)
    softmaxed = jax.nn.softmax(scores, axis=-1)
    softmaxed_low = softmaxed.astype(jnp.bfloat16)
    mixed = jnp.einsum(
        "hrm,mhe->rhe", softmaxed_low, value_heads, preferred_element_type=jnp.float32
    )
    return (
        mixed.astype(jnp.bfloat16).reshape(total_rows, heads_here * HD),
        softmaxed,
        softmaxed_low,
    )


def token_terms(rows, attended, weighted):
    hidden = rows.astype(jnp.float32) + attended
    inverse = lax.rsqrt(jnp.mean(hidden * hidden, axis=-1) + 1e-06)
    raw = jnp.sum(hidden * weighted[None, :], axis=-1)
    return (hidden, inverse, raw)


def goal_softmax(logits, live, visit):
    masked = jnp.where(live, logits, -1e30)
    top_value = jnp.max(masked)
    exponent = jnp.where(live, jnp.exp(masked - top_value), 0.0)
    log_total = top_value + jnp.log(jnp.sum(exponent))
    log_weight = jnp.where(live, logits - log_total, 0.0)
    visit_mass = jnp.where(live, visit.astype(jnp.float32), 0.0)
    target = visit_mass / jnp.sum(visit_mass)
    loss = -jnp.sum(target * log_weight)
    logit_grad = jnp.where(live, jnp.exp(log_weight) - target, 0.0)
    return (log_weight, loss, logit_grad)


def norm_grad(hidden, inverse, raw, tok_grad, weighted, model_width):
    factor = inverse * inverse * inverse * tok_grad * raw / model_width
    return ((inverse * tok_grad)[:, None] * weighted[None, :] - hidden * factor[:, None]).astype(
        jnp.bfloat16
    )


def body(dec_states, memory, counts, rank, visits, w_query, w_key, w_value, w_out, gain, w_score):
    width = w_query.shape[1]
    model_width = w_query.shape[0]
    heads_here = width // HD
    slot_here = dec_states.shape[1]
    memory_all = lax.all_gather(memory[0], "cand", axis=0, tiled=True)
    tactics = lax.all_gather(dec_states[0], "cand", axis=0, tiled=True)
    slots = tactics.shape[0]
    per_tactic = tactics.shape[1]
    rows = tactics.reshape(slots * per_tactic, model_width)
    total_rows = rows.shape[0]
    memory_rows = memory_all.shape[0]
    query = jnp.dot(rows, w_query, preferred_element_type=jnp.float32).astype(jnp.bfloat16)
    key = jnp.dot(memory_all, w_key, preferred_element_type=jnp.float32).astype(jnp.bfloat16)
    value = jnp.dot(memory_all, w_value, preferred_element_type=jnp.float32).astype(jnp.bfloat16)
    mixed, softmaxed, softmaxed_low = attend(query, key, value, heads_here)
    weighted = gain * w_score
    live = rank[0] < counts[0]
    first_slot = lax.axis_index("cand") * slot_here
    own_part = rounded(jnp.dot(mixed, w_out, preferred_element_type=jnp.float32))
    attended = lax.psum(own_part.astype(jnp.bfloat16), "cand").astype(jnp.float32)
    hidden, inverse, raw = token_terms(rows, attended, weighted)
    logits = jnp.mean((inverse * raw).reshape(slots, per_tactic), axis=1)
    log_weight, loss, logit_grad = goal_softmax(logits, live, visits[0])
    tok_grad = jnp.repeat(logit_grad / per_tactic, per_tactic, total_repeat_length=total_rows)
    hidden_grad = norm_grad(hidden, inverse, raw, tok_grad, weighted, model_width)
    mixed_grad = lax.dot_general(
        hidden_grad, w_out, (((1,), (1,)), ((), ())), preferred_element_type=jnp.float32
    ).astype(jnp.bfloat16)
    out_term = lax.dot_general(
        mixed, hidden_grad, (((0,), (0,)), ((), ())), preferred_element_type=jnp.float32
    )
    query_heads = query.reshape(total_rows, heads_here, HD)
    key_heads = key.reshape(memory_rows, heads_here, HD)
    value_heads = value.reshape(memory_rows, heads_here, HD)
    grad_heads = mixed_grad.reshape(total_rows, heads_here, HD)
    prob_grad = jnp.einsum(
        "rhe,mhe->hrm", grad_heads, value_heads, preferred_element_type=jnp.float32
    )
    delta = jnp.sum(softmaxed * prob_grad, axis=-1, keepdims=True)
    score_grad = (softmaxed * (prob_grad - delta) * HD ** (-0.5)).astype(jnp.bfloat16)
    query_grad = jnp.einsum(
        "hrm,mhe->rhe", score_grad, key_heads, preferred_element_type=jnp.float32
    )
    query_grad = query_grad.astype(jnp.bfloat16).reshape(total_rows, width)
    key_grad = jnp.einsum(
        "hrm,rhe->mhe", score_grad, query_heads, preferred_element_type=jnp.float32
    )
    key_grad = key_grad.astype(jnp.bfloat16).reshape(memory_rows, width)
    value_grad = jnp.einsum(
        "hrm,rhe->mhe", softmaxed_low, grad_heads, preferred_element_type=jnp.float32
    )
    value_grad = value_grad.astype(jnp.bfloat16).reshape(memory_rows, width)
    contract = (((0,), (0,)), ((), ()))
    query_term = rounded(
        lax.dot_general(rows, query_grad, contract, preferred_element_type=jnp.float32)
    )
    key_term = rounded(
        lax.dot_general(memory_all, key_grad, contract, preferred_element_type=jnp.float32)
    )
    value_term = rounded(
        lax.dot_general(memory_all, value_grad, contract, preferred_element_type=jnp.float32)
    )
    out_rounded = rounded(out_term)
    summed = (
        lax.psum_scatter(
            query_term.astype(jnp.bfloat16), "goal", scatter_dimension=0, tiled=True
        ).astype(jnp.float32),
        lax.psum_scatter(
            key_term.astype(jnp.bfloat16), "goal", scatter_dimension=0, tiled=True
        ).astype(jnp.float32),
        lax.psum_scatter(
            value_term.astype(jnp.bfloat16), "goal", scatter_dimension=0, tiled=True
        ).astype(jnp.float32),
        lax.psum_scatter(
            out_rounded.astype(jnp.bfloat16), "goal", scatter_dimension=1, tiled=True
        ).astype(jnp.float32),
    )
    own_log = lax.dynamic_slice_in_dim(log_weight, first_slot, slot_here, 0)
    return (
        own_log[None, :],
        loss[None],
        summed[0].astype(jnp.bfloat16),
        summed[1].astype(jnp.bfloat16),
        summed[2].astype(jnp.bfloat16),
        summed[3].astype(jnp.bfloat16),
    )


def solution(mesh):
    return jax.shard_map(
        body,
        mesh=mesh,
        in_specs=(
            P("goal", "cand", None, None),
            P("goal", "cand", None),
            P("goal"),
            P("goal", None),
            P("goal", None),
            P(None, "cand"),
            P(None, "cand"),
            P(None, "cand"),
            P("cand", None),
            P(),
            P(),
        ),
        out_specs=(
            P("goal", "cand"),
            P("goal"),
            P("goal", "cand"),
            P("goal", "cand"),
            P("goal", "cand"),
            P("cand", "goal"),
        ),
        check_vma=False,
    )
```

profile of v0, /device:TPU:0, one launch (start us, length us, event | category | flops | bytes accessed | tf_op | source)
XLA Modules:
  0.0 462.4 jit_solution(10033739450499721993)
XLA Ops:
  8.7 55.3 %all-gather.7.cloned.1.call-done = bf16[1,512,4096]{2,1,0:T(8,128)(2,1)} async-done(((bf16[1,32,4096]{2,1,0:T(8,128)(2,1)}), bf16[1,512,4096]{2,1,0:T(8,128)(2,1)}) %all-gather.7.cloned.1.call-update) | async-done | bytes 4194320 | tf_op jit(solution)/shard_map/all_gather | solution.py:66
  64.1 4.3 fusion.43
  70.1 57.1 %all-gather.5.cloned.1.call-done = bf16[1,32,24,4096]{3,2,0,1:T(8,128)(2,1)} async-done(((bf16[1,2,24,4096]{3,2,0,1:T(8,128)(2,1)}), bf16[1,32,24,4096]{3,2,0,1:T(8,128)(2,1)}) %all-gather.5.cloned.1.call-update) | async-done | bytes 6291472 | tf_op jit(solution)/shard_map/all_gather | solution.py:67
  127.2 5.2 %convolution_convert_fusion.6 = bf16[768,256]{0,1:T(8,128)(2,1)S(1)} fusion(bf16[768,4096]{1,0:T(8,128)(2,1)} %bitcast.128, bf16[4096,256]{1,0:T(8,128)(2,1)} %param.18), kind=kOutput, calls=%fused_computation.37 | convolution fusion | flops 1610809344 | bytes 8781824 | tf_op jit(solution)/shard_map/dot_general | solution.py:73
  132.5 4.6 fusion.64
  137.0 3.5 fusion.31
  140.6 4.5 convolution_convert_fusion
  146.4 120.6 %all-reduce.2.cloned.1.call-done = bf16[768,4096]{1,0:T(8,128)(2,1)} async-done(((bf16[768,4096]{1,0:T(8,128)(2,1)}), bf16[768,4096]{1,0:T(8,128)(2,1)}) %all-reduce.2.cloned.1.call-update) | async-done | bytes 6291472 | tf_op jit(solution)/shard_map/psum | solution.py:81
  267.0 6.6 %multiply_reduce_fusion.1 = (f32[768]{0:T(1024)S(1)}, f32[768]{0:T(1024)S(1)}) fusion(bf16[768,4096]{1,0:T(8,128)(2,1)} %all-reduce.2.cloned.1.call-done, bf16[1,32,24,4096]{3,2,0,1:T(8,128)(2,1)} %all-gather.5.cloned.1.call-done, f32[4096]{0:T(1024)S(1)} %mul.95), kind=kLoop, calls=%fused_computation.4 | loop fusion | flops 22018560 | bytes 12605440 | tf_op jit(solution)/shard_map/reduce_sum | solution.py:36
  279.4 20.0 %fusion.51 = (f32[768]{0:T(1024)S(1)}, f32[768]{0:T(1024)S(1)}) fusion(f32[768]{0:T(1024)S(1)} %get-tuple-element.36, pred[768]{0:T(1024)(128)(4,1)S(1)} %copy-done.35, pred[768]{0:T(1024)(128)(4,1)S(1)} %copy-done.34, pred[768]{0:T(1024)(128)(4,1)S(1)} %copy-done.33, pred[768]{0:T(1024)(128)(4,1)S(1)} %copy-done.32, pred[768]{0:T(1024)(128)(4,1)S(1)} %copy-done.31, ...), kind=kLoop, calls=%fused_computation.49 | loop fusion | flops 26112 | bytes 33152 | tf_op jit(solution)/shard_map/mul | solution.py:56
  299.4 7.0 %subtract_convert_fusion = bf16[768,4096]{1,0:T(8,128)(2,1)S(1)} fusion(bf16[768,4096]{1,0:T(8,128)(2,1)} %all-reduce.2.cloned.1.call-done, f32[768]{0:T(1024)S(1)} %fusion.50, f32[768]{0:T(1024)S(1)} %get-tuple-element.40, f32[4096]{0:T(1024)S(1)} %mul.95, bf16[1,32,24,4096]{3,2,0,1:T(8,128)(2,1)} %all-gather.5.cloned.1.call-done), kind=kLoop, calls=%fused_computation.2 | loop fusion | flops 22020096 | bytes 18896896 | tf_op jit(solution)/shard_map/convert_element_type | solution.py:56
  306.4 1.8 convolution_convert_fusion.5
  308.3 4.2 fusion.37
  312.5 2.6 fusion.6
  315.2 3.7 fusion.65
  318.9 10.4 %fusion.34 = bf16[4,64,512]{2,1,0:T(8,128)(2,1)S(1)} fusion(bf16[768,4,64]{0,2,1:T(8,128)(2,1)S(1)} %bitcast.138, f32[4,768,512]{1,2,0:T(8,128)} %fusion.65, f32[4,768,512]{1,2,0:T(8,128)} %get-tuple-element.80, f32[4,768]{1,0:T(4,128)} %copy-done.42), kind=kOutput, calls=%fused_computation.38 | convolution fusion | flops 212471296 | bytes 13250560 | tf_op jit(solution)/shard_map/hrm,rhe->mhe/dot_general | solution.py:106
  329.3 4.9 %fusion.5 = bf16[4096,256]{0,1:T(8,128)(2,1)} fusion(bf16[512,256]{0,1:T(8,128)(2,1)S(1)} %bitcast.142, bf16[1,512,4096]{2,1,0:T(8,128)(2,1)} %all-gather.7.cloned.1.call-done), kind=kOutput, calls=%fused_computation.18 | convolution fusion | flops 1074790400 | bytes 6553600 | tf_op jit(solution)/shard_map/dot_general | solution.py:119
  334.5 10.5 %fusion.28 = bf16[4,64,768]{2,1,0:T(8,128)(2,1)S(1)} fusion(bf16[512,4,64]{0,2,1:T(8,128)(2,1)S(1)} %bitcast.141, f32[4,768,512]{1,2,0:T(8,128)} %fusion.65, f32[4,768,512]{1,2,0:T(8,128)} %get-tuple-element.80, f32[4,768]{1,0:T(4,128)S(1)} %copy-done.44), kind=kOutput, calls=%fused_computation.34 | convolution fusion | flops 212536832 | bytes 13250560 | tf_op jit(solution)/shard_map/hrm,mhe->rhe/dot_general | solution.py:102
  345.0 6.0 %fusion.4 = bf16[4096,256]{0,1:T(8,128)(2,1)} fusion(bf16[768,256]{0,1:T(8,128)(2,1)S(1)} %bitcast.139, bf16[768,4096]{1,0:T(8,128)(2,1)} %bitcast.129), kind=kOutput, calls=%fused_computation.17 | convolution fusion | flops 1611661312 | bytes 8781824 | tf_op jit(solution)/shard_map/dot_general | solution.py:116
  351.1 6.0 %convolution_convert_fusion.3 = bf16[256,4096]{1,0:T(8,128)(2,1)} fusion(bf16[768,256]{0,1:T(8,128)(2,1)S(1)} %bitcast.131, bf16[768,4096]{1,0:T(8,128)(2,1)} %copy-done.1), kind=kOutput, calls=%fused_computation.15 | convolution fusion | flops 1611661312 | bytes 8781824 | tf_op jit(solution)/shard_map/dot_general | solution.py:90
  358.9 1.8 copy.38
  360.7 23.2 %reduce-scatter.7.cloned.1.call-done = bf16[512,256]{0,1:T(8,128)(2,1)} async-done(((bf16[4096,256]{0,1:T(8,128)(2,1)}), bf16[512,256]{0,1:T(8,128)(2,1)}) %reduce-scatter.7.cloned.1.call-update) | async-done | bytes 262160 | tf_op jit(solution)/shard_map/reduce_scatter | solution.py:129
  385.7 33.1 %reduce-scatter.5.cloned.1.call-done = bf16[512,256]{0,1:T(8,128)(2,1)} async-done(((bf16[4096,256]{0,1:T(8,128)(2,1)}), bf16[512,256]{0,1:T(8,128)(2,1)}) %reduce-scatter.5.cloned.1.call-update) | async-done | bytes 262160 | tf_op jit(solution)/shard_map/reduce_scatter | solution.py:126
  420.6 33.8 %reduce-scatter.11.cloned.1.call-done = bf16[256,512]{1,0:T(8,128)(2,1)} async-done(((bf16[256,4096]{1,0:T(8,128)(2,1)}), bf16[256,512]{1,0:T(8,128)(2,1)}) %reduce-scatter.11.cloned.1.call-update) | async-done | bytes 262160 | tf_op jit(solution)/shard_map/reduce_scatter | solution.py:135
  (120 shorter events, 13.1 us)
Async XLA Ops:
  7.2 133.4 %copy-start = (bf16[256,4096]{1,0:T(8,128)(2,1)S(1)}, bf16[256,4096]{1,0:T(8,128)(2,1)}, u32[]{:S(2)}) copy-start(bf16[256,4096]{1,0:T(8,128)(2,1)} %param.21) | copy-start | bytes 6291460
  7.2 56.9 %all-gather.7.cloned.1.call-start = ((), (), s32[]{:S(2)}) async-start(), calls=%async_computation.10 | async-start | bytes 4456448 | tf_op jit(solution)/shard_map/all_gather | solution.py:66
  7.9 119.3 %all-gather.5.cloned.1.call-start = ((), (), s32[]{:S(2)}) async-start(), calls=%async_computation.9 | async-start | bytes 6684672 | tf_op jit(solution)/shard_map/all_gather | solution.py:67
  8.7 258.4 %all-reduce.2.cloned.1.call-start = ((), (), s32[]{:S(2)}) async-start(), calls=%async_computation.4 | async-start | bytes 12582912 | tf_op jit(solution)/shard_map/psum | solution.py:81
  145.1 213.9 %reduce-scatter.9.cloned.1.call-start = ((), (), s32[]{:S(2)}) async-start(), calls=%async_computation.7 | async-start | bytes 2359296 | tf_op jit(solution)/shard_map/reduce_scatter | solution.py:132
  146.0 133.1 %copy-start.5 = (pred[768]{0:T(1024)(128)(4,1)S(1)}, pred[768]{0:T(1024)(128)(4,1)}, u32[]{:S(2)}) copy-start(pred[768]{0:T(1024)(128)(4,1)} %constant.197) | copy-start | bytes 2308
  146.0 133.1 %copy-start.6 = (pred[768]{0:T(1024)(128)(4,1)S(1)}, pred[768]{0:T(1024)(128)(4,1)}, u32[]{:S(2)}) copy-start(pred[768]{0:T(1024)(128)(4,1)} %constant.196) | copy-start | bytes 2308
  146.0 133.1 %copy-start.7 = (pred[768]{0:T(1024)(128)(4,1)S(1)}, pred[768]{0:T(1024)(128)(4,1)}, u32[]{:S(2)}) copy-start(pred[768]{0:T(1024)(128)(4,1)} %constant.195) | copy-start | bytes 2308
  146.0 133.1 %copy-start.8 = (pred[768]{0:T(1024)(128)(4,1)S(1)}, pred[768]{0:T(1024)(128)(4,1)}, u32[]{:S(2)}) copy-start(pred[768]{0:T(1024)(128)(4,1)} %constant.194) | copy-start | bytes 2308
  146.0 133.1 %copy-start.9 = (pred[768]{0:T(1024)(128)(4,1)S(1)}, pred[768]{0:T(1024)(128)(4,1)}, u32[]{:S(2)}) copy-start(pred[768]{0:T(1024)(128)(4,1)} %constant.193) | copy-start | bytes 2308
  146.1 133.1 %copy-start.10 = (pred[768]{0:T(1024)(128)(4,1)S(1)}, pred[768]{0:T(1024)(128)(4,1)}, u32[]{:S(2)}) copy-start(pred[768]{0:T(1024)(128)(4,1)} %constant.192) | copy-start | bytes 2308
  146.1 133.1 %copy-start.11 = (pred[768]{0:T(1024)(128)(4,1)S(1)}, pred[768]{0:T(1024)(128)(4,1)}, u32[]{:S(2)}) copy-start(pred[768]{0:T(1024)(128)(4,1)} %constant.191) | copy-start | bytes 2308
  146.1 133.1 %copy-start.12 = (pred[768]{0:T(1024)(128)(4,1)S(1)}, pred[768]{0:T(1024)(128)(4,1)}, u32[]{:S(2)}) copy-start(pred[768]{0:T(1024)(128)(4,1)} %constant.190) | copy-start | bytes 2308
  146.1 133.1 %copy-start.13 = (pred[768]{0:T(1024)(128)(4,1)S(1)}, pred[768]{0:T(1024)(128)(4,1)}, u32[]{:S(2)}) copy-start(pred[768]{0:T(1024)(128)(4,1)} %constant.189) | copy-start | bytes 2308
  146.1 133.1 %copy-start.14 = (pred[768]{0:T(1024)(128)(4,1)S(1)}, pred[768]{0:T(1024)(128)(4,1)}, u32[]{:S(2)}) copy-start(pred[768]{0:T(1024)(128)(4,1)} %constant.188) | copy-start | bytes 2308
  146.1 133.1 %copy-start.15 = (pred[768]{0:T(1024)(128)(4,1)S(1)}, pred[768]{0:T(1024)(128)(4,1)}, u32[]{:S(2)}) copy-start(pred[768]{0:T(1024)(128)(4,1)} %constant.187) | copy-start | bytes 2308
  146.1 133.1 %copy-start.16 = (pred[768]{0:T(1024)(128)(4,1)S(1)}, pred[768]{0:T(1024)(128)(4,1)}, u32[]{:S(2)}) copy-start(pred[768]{0:T(1024)(128)(4,1)} %constant.186) | copy-start | bytes 2308
  146.1 133.1 %copy-start.17 = (pred[768]{0:T(1024)(128)(4,1)S(1)}, pred[768]{0:T(1024)(128)(4,1)}, u32[]{:S(2)}) copy-start(pred[768]{0:T(1024)(128)(4,1)} %constant.185) | copy-start | bytes 2308
  146.2 133.1 %copy-start.18 = (pred[768]{0:T(1024)(128)(4,1)S(1)}, pred[768]{0:T(1024)(128)(4,1)}, u32[]{:S(2)}) copy-start(pred[768]{0:T(1024)(128)(4,1)} %constant.184) | copy-start | bytes 2308
  146.2 133.1 %copy-start.19 = (pred[768]{0:T(1024)(128)(4,1)S(1)}, pred[768]{0:T(1024)(128)(4,1)}, u32[]{:S(2)}) copy-start(pred[768]{0:T(1024)(128)(4,1)} %constant.183) | copy-start | bytes 2308
  146.2 133.1 %copy-start.20 = (pred[768]{0:T(1024)(128)(4,1)S(1)}, pred[768]{0:T(1024)(128)(4,1)}, u32[]{:S(2)}) copy-start(pred[768]{0:T(1024)(128)(4,1)} %constant.182) | copy-start | bytes 2308
  315.2 68.7 %reduce-scatter.7.cloned.1.call-start = ((), (), s32[]{:S(2)}) async-start(), calls=%async_computation.6 | async-start | bytes 2359296 | tf_op jit(solution)/shard_map/reduce_scatter | solution.py:129
  334.2 84.6 %reduce-scatter.5.cloned.1.call-start = ((), (), s32[]{:S(2)}) async-start(), calls=%async_computation.5 | async-start | bytes 2359296 | tf_op jit(solution)/shard_map/reduce_scatter | solution.py:126
  351.0 103.4 %reduce-scatter.11.cloned.1.call-start = ((), (), s32[]{:S(2)}) async-start(), calls=%async_computation.8 | async-start | bytes 2359296 | tf_op jit(solution)/shard_map/reduce_scatter | solution.py:135
  (28 other events, 2361.3 us)
Sparse Core Ops, SparseCore 0:
  10.2 53.8 all-gather.6
  66.2 60.9 all-gather.4
  145.2 121.8 all-reduce.1
  315.3 33.6 reduce-scatter.8
  351.4 32.4 reduce-scatter.6
  386.3 32.4 reduce-scatter.4
  421.9 32.4 reduce-scatter.10
where the time goes:
time: 463 us; the launch traced here: 462 us
  waiting for transfers between devices  325 us (70%)
  matrix products  73.4 us (16%)
  other arithmetic  36.8 us (8%)
  between operations  18.7 us (4%)
  local copies, waits for them, and re-layouts  8.22 us (2%)
    psum x1, waiting for transfers between devices, body(): lax.psum(own_part.astype(jnp.bfloat16), 'cand').astype(jnp.float32)  121 us
    all_gather x1, waiting for transfers between devices, body(): tactics = lax.all_gather(dec_states[0], 'cand', axis=0, tiled=True)  57.1 us
    all_gather x1, waiting for transfers between devices, body(): memory_all = lax.all_gather(memory[0], 'cand', axis=0, tiled=True)  55.3 us
    reduce_scatter x1, waiting for transfers between devices, body(): lax.psum_scatter(out_rounded.astype(jnp.bfloat16), 'goal', scatter_dimens...  33.8 us
    reduce_scatter x1, waiting for transfers between devices, body(): lax.psum_scatter(query_term.astype(jnp.bfloat16), 'goal', scatter_dimensi...  33.1 us
    reduce_scatter x1, waiting for transfers between devices, body(): lax.psum_scatter(key_term.astype(jnp.bfloat16), 'goal', scatter_dimension...  23.2 us
    mul x1, other arithmetic, norm_grad(): inverse * tok_grad  20 us
    dot_general x1, matrix products, body(): jnp.einsum('hrm,mhe->rhe', score_grad, key_heads, preferred_element_type=...  10.5 us
  transfers between devices with their start and end apart: 7, of which 6 were waited for; matrix products, arithmetic and copies ran while one was open for 12% of the time, Pallas kernels for 0%

commit v1 on v0

--- a/solution.py
+++ b/solution.py
@@ -4,6 +4,79 @@
 from jax.sharding import PartitionSpec as P
 
 HD = 64
+
+
+CAND_MASKS = (4, 12, 1, 3)
+PART_ORDERS = ((0, 1, 2, 3), (1, 0, 3, 2), (2, 3, 0, 1), (3, 2, 1, 0))
+
+
+def swap(values, axis, size, mask):
+    return lax.ppermute(values, axis, [(i, i ^ mask) for i in range(size)])
+
+
+def pair_bits(coordinate):
+    high = coordinate >> 1
+    return ((coordinate & 1) ^ high, high)
+
+
+def slot_order():
+    order = []
+    for position in range(16):
+        bits = [(position >> i) & 1 for i in range(4)]
+        x = bits[0] ^ (3 * bits[1])
+        y = bits[2] ^ (3 * bits[3])
+        order.append(4 * x + y)
+    return order
+
+
+def gather_cand(own, bits):
+    parts = [part[None, None, None, None] for part in jnp.split(own, 4, axis=1)]
+    for step in range(4):
+        parts = lax.optimization_barrier(parts)
+        others = [
+            swap(part, "cand", 16, CAND_MASKS[order[step]])
+            for part, order in zip(parts, PART_ORDERS)
+        ]
+        others = lax.optimization_barrier(others)
+        merged = []
+        for part, other, order in zip(parts, others, PART_ORDERS):
+            bit = bits[order[step]]
+            low = jnp.where(bit == 0, part, other)
+            high = jnp.where(bit == 0, other, part)
+            merged.append(jnp.concatenate([low, high], axis=3 - order[step]))
+        parts = merged
+    return parts
+
+
+def sum_goals(terms, core, low_bit, high_bit):
+    blocks = terms.reshape(terms.shape[0], 4, 2, 512, 256)
+    send = jnp.where(core == 0, blocks[:, :, 1], blocks[:, :, 0])
+    keep = jnp.where(core == 0, blocks[:, :, 0], blocks[:, :, 1])
+    both = plus(keep, swap(send, "goal", 8, 1))
+    halves = []
+    for part, first in ((both[:, :, :256], 0), (both[:, :, 256:], 1)):
+        lines = jnp.stack([part[:, 0], part[:, 1], part[:, 3], part[:, 2]], axis=1)
+        lines = lines.reshape(terms.shape[0], 2, 2, 256, 256)
+        halves.append((lines, first))
+    bits = (low_bit, high_bit)
+    masks = (2, 6)
+    kept = []
+    for lines, first in halves:
+        zero, one = (lines[:, :, 0], lines[:, :, 1]) if first == 0 else (lines[:, 0], lines[:, 1])
+        bit = bits[first]
+        other = swap(jnp.where(bit == 0, one, zero), "goal", 8, masks[first])
+        kept.append(plus(jnp.where(bit == 0, zero, one), other))
+    done = []
+    for lines, second in zip(kept, (1, 0)):
+        zero, one = lines[:, 0], lines[:, 1]
+        bit = bits[second]
+        other = swap(jnp.where(bit == 0, one, zero), "goal", 8, masks[second])
+        done.append(plus(jnp.where(bit == 0, zero, one), other))
+    return jnp.concatenate(done, axis=1)
+
+
+def plus(left, right):
+    return (left.astype(jnp.float32) + right.astype(jnp.float32)).astype(jnp.bfloat16)
 
 
 def rounded(values):
@@ -63,11 +136,24 @@
     model_width = w_query.shape[0]
     heads_here = width // HD
     slot_here = dec_states.shape[1]
-    memory_all = lax.all_gather(memory[0], "cand", axis=0, tiled=True)
-    tactics = lax.all_gather(dec_states[0], "cand", axis=0, tiled=True)
-    slots = tactics.shape[0]
-    per_tactic = tactics.shape[1]
-    rows = tactics.reshape(slots * per_tactic, model_width)
+    cand = lax.axis_index("cand")
+    goal = lax.axis_index("goal")
+    bits = pair_bits(cand >> 2) + pair_bits(cand & 3)
+    per_tactic = dec_states.shape[2]
+    own_rows = slot_here * per_tactic
+    own = jnp.concatenate([dec_states[0].reshape(own_rows, model_width), memory[0]], axis=0)
+    parts = gather_cand(own, bits)
+    slots = 16 * slot_here
+    rows = jnp.concatenate(
+        [part[..., :own_rows, :].reshape(16 * own_rows, -1) for part in parts], axis=1
+    )
+    memory_all = jnp.concatenate(
+        [part[..., own_rows:, :].reshape(16 * memory.shape[1], -1) for part in parts], axis=1
+    )
+    order = jnp.array([c * slot_here + s for c in slot_order() for s in range(slot_here)], jnp.int32)
+    pick = order[:, None] == jnp.arange(slots, dtype=jnp.int32)[None, :]
+    rank_here = jnp.sum(jnp.where(pick, rank, 0), axis=1)
+    visits_here = jnp.sum(jnp.where(pick, visits, 0), axis=1)
     total_rows = rows.shape[0]
     memory_rows = memory_all.shape[0]
     query = jnp.dot(rows, w_query, preferred_element_type=jnp.float32).astype(jnp.bfloat16)
@@ -75,20 +161,19 @@
     value = jnp.dot(memory_all, w_value, preferred_element_type=jnp.float32).astype(jnp.bfloat16)
     mixed, softmaxed, softmaxed_low = attend(query, key, value, heads_here)
     weighted = gain * w_score
-    live = rank[0] < counts[0]
-    first_slot = lax.axis_index("cand") * slot_here
+    live = rank_here < counts[0]
     own_part = rounded(jnp.dot(mixed, w_out, preferred_element_type=jnp.float32))
     attended = lax.psum(own_part.astype(jnp.bfloat16), "cand").astype(jnp.float32)
     hidden, inverse, raw = token_terms(rows, attended, weighted)
     logits = jnp.mean((inverse * raw).reshape(slots, per_tactic), axis=1)
-    log_weight, loss, logit_grad = goal_softmax(logits, live, visits[0])
+    log_weight, loss, logit_grad = goal_softmax(logits, live, visits_here)
     tok_grad = jnp.repeat(logit_grad / per_tactic, per_tactic, total_repeat_length=total_rows)
     hidden_grad = norm_grad(hidden, inverse, raw, tok_grad, weighted, model_width)
     mixed_grad = lax.dot_general(
         hidden_grad, w_out, (((1,), (1,)), ((), ())), preferred_element_type=jnp.float32
     ).astype(jnp.bfloat16)
     out_term = lax.dot_general(
-        mixed, hidden_grad, (((0,), (0,)), ((), ())), preferred_element_type=jnp.float32
+        hidden_grad, mixed, (((0,), (0,)), ((), ())), preferred_element_type=jnp.float32
     )
     query_heads = query.reshape(total_rows, heads_here, HD)
     key_heads = key.reshape(memory_rows, heads_here, HD)
@@ -112,38 +197,26 @@
     )
     value_grad = value_grad.astype(jnp.bfloat16).reshape(memory_rows, width)
     contract = (((0,), (0,)), ((), ()))
-    query_term = rounded(
-        lax.dot_general(rows, query_grad, contract, preferred_element_type=jnp.float32)
-    )
-    key_term = rounded(
-        lax.dot_general(memory_all, key_grad, contract, preferred_element_type=jnp.float32)
-    )
-    value_term = rounded(
-        lax.dot_general(memory_all, value_grad, contract, preferred_element_type=jnp.float32)
-    )
-    out_rounded = rounded(out_term)
-    summed = (
-        lax.psum_scatter(
-            query_term.astype(jnp.bfloat16), "goal", scatter_dimension=0, tiled=True
-        ).astype(jnp.float32),
-        lax.psum_scatter(
-            key_term.astype(jnp.bfloat16), "goal", scatter_dimension=0, tiled=True
-        ).astype(jnp.float32),
-        lax.psum_scatter(
-            value_term.astype(jnp.bfloat16), "goal", scatter_dimension=0, tiled=True
-        ).astype(jnp.float32),
-        lax.psum_scatter(
-            out_rounded.astype(jnp.bfloat16), "goal", scatter_dimension=1, tiled=True
-        ).astype(jnp.float32),
-    )
-    own_log = lax.dynamic_slice_in_dim(log_weight, first_slot, slot_here, 0)
+    query_term = lax.dot_general(rows, query_grad, contract, preferred_element_type=jnp.float32)
+    key_term = lax.dot_general(memory_all, key_grad, contract, preferred_element_type=jnp.float32)
+    value_term = lax.dot_general(
+        memory_all, value_grad, contract, preferred_element_type=jnp.float32
+    )
+    core = goal & 1
+    low_bit, high_bit = pair_bits(goal >> 1)
+    first = jnp.stack([out_term.astype(jnp.bfloat16), value_term.astype(jnp.bfloat16)])
+    second = jnp.stack([query_term.astype(jnp.bfloat16), key_term.astype(jnp.bfloat16)])
+    first = sum_goals(first, core, low_bit, high_bit)
+    second = sum_goals(second, core, low_bit, high_bit)
+    own_slots = cand * slot_here + jnp.arange(slot_here, dtype=jnp.int32)
+    own_log = jnp.sum(jnp.where(own_slots[:, None] == order[None, :], log_weight[None, :], 0.0), axis=1)
     return (
         own_log[None, :],
         loss[None],
-        summed[0].astype(jnp.bfloat16),
-        summed[1].astype(jnp.bfloat16),
-        summed[2].astype(jnp.bfloat16),
-        summed[3].astype(jnp.bfloat16),
+        second[0],
+        second[1],
+        first[1],
+        first[0].T,
     )
 
 

time: 463 us -> 392 us (0.85); the launches traced: 462 us -> 386 us
  waiting for transfers between devices: 325 us -> 191 us
  starting transfers between devices: 0.68 us -> 32 us
  other arithmetic: 36.8 us -> 64.4 us
  matrix products: 73.4 us -> 66.7 us
    all_gather x2 -> x0, waiting for transfers between devices: 112 us -> none  [the longest x1 57.1 us: body(): tactics = lax.all_gather(dec_states[0], 'cand', axis=0, tiled=True)]
    reduce_scatter x4 -> x0, waiting for transfers between devices: 90.2 us -> none  [the longest x1 33.8 us: body(): lax.psum_scatter(out_rounded.astype(jnp.bfloat16), 'goal', scatter_dimens...]
    ppermute x0 -> x26, waiting for transfers between devices: none -> 71.4 us  [swap(): return lax.ppermute(values, axis, [(i, i ^ mask) for i in range(size)])]
    ppermute x0 -> x26, starting transfers between devices: none -> 32 us  [swap(): return lax.ppermute(values, axis, [(i, i ^ mask) for i in range(size)])]
    convert_element_type x0 -> x10, other arithmetic: none -> 7.73 us  [plus(): (left.astype(jnp.float32) + right.astype(jnp.float32)).astype(jnp.bfloat16)]
    select_n x0 -> x24, other arithmetic: none -> 6.26 us  [the longest x2 3.09 us: sum_goals(): send = jnp.where(core == 0, blocks[:, :, 1], blocks[:, :, 0])]
    unnamed x93 -> x83, local copies, waits for them, and re-layouts: 6.16 us -> 9.29 us
  transfers between devices with their start and end apart: 7 -> 27, of which waited for: 6 -> 18; matrix products, arithmetic and copies ran while one was open for 12% -> 6% of each run, Pallas kernels for 0% -> 0%
where the time goes in v1:
time: 392 us; the launch traced here: 386 us
  waiting for transfers between devices  191 us (49%)
  matrix products  66.7 us (17%)
  other arithmetic  64.4 us (16%)
  starting transfers between devices  32 us (8%)
  between operations  19.1 us (5%)
  local copies, waits for them, and re-layouts  12.6 us (3%)
    psum x1, waiting for transfers between devices, body(): lax.psum(own_part.astype(jnp.bfloat16), 'cand').astype(jnp.float32)  120 us
    ppermute x26, waiting for transfers between devices, swap(): return lax.ppermute(values, axis, [(i, i ^ mask) for i in range(size)])  71.4 us
    ppermute x26, starting transfers between devices, swap(): return lax.ppermute(values, axis, [(i, i ^ mask) for i in range(size)])  32 us
    mul x1, other arithmetic, norm_grad(): inverse * tok_grad  20.7 us
    dot_general x1, matrix products, body(): jnp.einsum('hrm,mhe->rhe', score_grad, key_heads, preferred_element_type=...  10.3 us
    dot_general x1, matrix products, body(): jnp.einsum('hrm,rhe->mhe', score_grad, query_heads, preferred_element_typ...  10.1 us
    unnamed x83, local copies, waits for them, and re-layouts  9.29 us
  transfers between devices with their start and end apart: 27, of which 18 were waited for; matrix products, arithmetic and copies ran while one was open for 6% of the time, Pallas kernels for 0%

profile of v1, /device:TPU:0, one launch (start us, length us, event | category | flops | bytes accessed | tf_op | source)
XLA Modules:
  0.0 385.9 jit_solution(15990609523846366918)
XLA Ops:
  24.1 5.3 %collective-permute-done.4 = bf16[1,1,1,2,80,1024]{5,4,3,2,1,0:T(8,128)(2,1)S(1)} collective-permute-done((bf16[1,1,1,2,80,1024]{5,4,3,2,1,0:T(8,128)(2,1)S(1)}, bf16[1,1,1,2,80,1024]{5,4,3,2,1,0:T(8,128)(2,1)S(1)}, u32[]{:S(2)}, u32[]{:S(2)}) %collective-permute-start.4) | collective-permute-done | bytes 327712 | tf_op jit(solution)/shard_map/ppermute | solution.py:14
  37.1 8.1 %collective-permute-done.10 = bf16[2,2,1,1,80,1024]{5,4,3,2,1,0:T(8,128)(2,1)S(1)} collective-permute-done((bf16[2,2,1,1,80,1024]{5,4,3,2,1,0:T(8,128)(2,1)S(1)}, bf16[2,2,1,1,80,1024]{5,4,3,2,1,0:T(8,128)(2,1)S(1)}, u32[]{:S(2)}, u32[]{:S(2)}) %collective-permute-start.10) | collective-permute-done | bytes 655392 | tf_op jit(solution)/shard_map/ppermute | solution.py:14
  54.9 22.6 %collective-permute-done.12 = bf16[1,2,2,2,80,1024]{5,4,3,2,1,0:T(8,128)(2,1)S(1)} collective-permute-done((bf16[1,2,2,2,80,1024]{5,4,3,2,1,0:T(8,128)(2,1)S(1)}, bf16[1,2,2,2,80,1024]{5,4,3,2,1,0:T(8,128)(2,1)S(1)}, u32[]{:S(2)}, u32[]{:S(2)}) %collective-permute-start.12) | collective-permute-done | bytes 1310752 | tf_op jit(solution)/shard_map/ppermute | solution.py:14
  88.7 2.8 convolution_convert_fusion.6
  91.6 5.7 %fusion.90 = (f32[4,768]{1,0:T(4,128)S(1)}, f32[4,768,512]{1,2,0:T(8,128)}) fusion(bf16[768,4,64]{0,2,1:T(8,128)(2,1)S(1)} %bitcast.262, bf16[512,4,64]{0,2,1:T(8,128)(2,1)} %bitcast.265), kind=kOutput, calls=%fused_computation.210 | convolution fusion | flops 206045696 | bytes 6959104 | tf_op jit(solution)/shard_map/sub | solution.py:95
  97.3 3.6 fusion.34
  100.9 4.4 %convolution_convert_fusion = bf16[768,4096]{1,0:T(8,128)(2,1)} fusion(bf16[768,256]{0,1:T(8,128)(2,1)S(1)} %bitcast.251, bf16[256,4096]{1,0:T(8,128)(2,1)S(1)} %copy-done), kind=kOutput, calls=%fused_computation.6 | convolution fusion | flops 1613758464 | bytes 8781824 | tf_op jit(solution)/shard_map/dot_general | solution.py:165
  108.1 119.8 %all-reduce.2.cloned.1.call-done = bf16[768,4096]{1,0:T(8,128)(2,1)} async-done(((bf16[768,4096]{1,0:T(8,128)(2,1)}), bf16[768,4096]{1,0:T(8,128)(2,1)}) %all-reduce.2.cloned.1.call-update) | async-done | bytes 6291472 | tf_op jit(solution)/shard_map/psum | solution.py:166
  227.9 6.4 %multiply_reduce_fusion.1 = (f32[768]{0:T(1024)S(1)}, f32[768]{0:T(1024)S(1)}) fusion(bf16[768,4096]{1,0:T(8,128)(2,1)} %all-reduce.2.cloned.1.call-done, bf16[768,1024]{1,0:T(8,128)(2,1)} %bitcast.218, bf16[768,1024]{1,0:T(8,128)(2,1)} %bitcast.214, bf16[768,1024]{1,0:T(8,128)(2,1)} %bitcast.210, bf16[768,1024]{1,0:T(8,128)(2,1)} %bitcast.206, f32[4096]{0:T(1024)S(1)} %mul.96), kind=kLoop, calls=%fused_computation.4 | loop fusion | flops 44038656 | bytes 12605440 | tf_op jit(solution)/shard_map/reduce_sum | solution.py:109
  246.4 20.7 %fusion.73 = (f32[768]{0:T(1024)S(1)}, f32[768]{0:T(1024)S(1)}) fusion(f32[768]{0:T(1024)} %copy-done.24, pred[768]{0:T(1024)(128)(4,1)} %constant.177, pred[768]{0:T(1024)(128)(4,1)} %constant.178, pred[768]{0:T(1024)(128)(4,1)} %constant.179, pred[768]{0:T(1024)(128)(4,1)} %constant.180, pred[768]{0:T(1024)(128)(4,1)} %constant.181, ...), kind=kLoop, calls=%fused_computation.183 | loop fusion | flops 26112 | bytes 33152 | tf_op jit(solution)/shard_map/mul | solution.py:129
  267.7 7.1 %subtract_convert_fusion = bf16[768,4096]{1,0:T(8,128)(2,1)S(1)} fusion(bf16[768,4096]{1,0:T(8,128)(2,1)} %all-reduce.2.cloned.1.call-done, f32[768]{0:T(1024)S(1)} %fusion.72, f32[768]{0:T(1024)S(1)} %get-tuple-element.100, f32[4096]{0:T(1024)S(1)} %mul.96, bf16[768,1024]{1,0:T(8,128)(2,1)} %bitcast.219, bf16[768,1024]{1,0:T(8,128)(2,1)} %bitcast.215, ...), kind=kLoop, calls=%fused_computation.2 | loop fusion | flops 44040192 | bytes 18896896 | tf_op jit(solution)/shard_map/convert_element_type | solution.py:129
  274.8 3.3 convolution_convert_fusion.3
  281.8 3.7 fusion.91
  285.5 10.3 %fusion.31 = bf16[4,64,768]{2,1,0:T(8,128)(2,1)S(1)} fusion(bf16[512,4,64]{0,2,1:T(8,128)(2,1)S(1)} %bitcast.266, f32[4,768,512]{1,2,0:T(8,128)} %fusion.91, f32[4,768,512]{1,2,0:T(8,128)} %get-tuple-element.197, f32[4,768]{1,0:T(4,128)S(1)} %copy-done.38), kind=kOutput, calls=%fused_computation.69 | convolution fusion | flops 212536832 | bytes 13250560 | tf_op jit(solution)/shard_map/hrm,mhe->rhe/dot_general | solution.py:187
  295.8 10.1 %fusion.37 = bf16[4,64,512]{2,1,0:T(8,128)(2,1)} fusion(bf16[768,4,64]{0,2,1:T(8,128)(2,1)S(1)} %bitcast.263, f32[4,768,512]{1,2,0:T(8,128)} %fusion.91, f32[4,768,512]{1,2,0:T(8,128)} %get-tuple-element.197, f32[4,768]{1,0:T(4,128)S(1)} %copy-done.38), kind=kOutput, calls=%fused_computation.73 | convolution fusion | flops 212471296 | bytes 13250560 | tf_op jit(solution)/shard_map/hrm,rhe->mhe/dot_general | solution.py:191
  305.9 3.3 convolution_convert_fusion.1
  312.7 4.5 %convolution_convert_fusion.2 = bf16[4096,256]{1,0:T(8,128)(2,1)S(1)} fusion(bf16[512,256]{0,1:T(8,128)(2,1)S(1)} %bitcast.267, bf16[512,1024]{1,0:T(8,128)(2,1)S(1)} %bitcast.250, bf16[512,1024]{1,0:T(8,128)(2,1)S(1)} %bitcast.246, bf16[512,1024]{1,0:T(8,128)(2,1)S(1)} %bitcast.242, bf16[512,1024]{1,0:T(8,128)(2,1)S(1)} %bitcast.238), kind=kOutput, calls=%fused_computation.15 | convolution fusion | flops 1091567616 | bytes 6553600 | tf_op jit(solution)/shard_map/dot_general | solution.py:201
  317.2 6.1 %convolution_convert_fusion.4 = bf16[4096,256]{1,0:T(8,128)(2,1)S(1)} fusion(bf16[768,256]{0,1:T(8,128)(2,1)S(1)} %bitcast.264, bf16[768,1024]{1,0:T(8,128)(2,1)S(1)} %bitcast.220, bf16[768,1024]{1,0:T(8,128)(2,1)S(1)} %bitcast.216, bf16[768,1024]{1,0:T(8,128)(2,1)S(1)} %bitcast.212, bf16[768,1024]{1,0:T(8,128)(2,1)S(1)} %bitcast.208), kind=kOutput, calls=%fused_computation.17 | convolution fusion | flops 1636827136 | bytes 8781824 | tf_op jit(solution)/shard_map/dot_general | solution.py:200
  340.9 8.7 %collective-permute-done.22 = bf16[2,2,256,256]{3,2,0,1:T(8,128)(2,1)S(1)} collective-permute-done((bf16[2,2,256,256]{3,2,0,1:T(8,128)(2,1)S(1)}, bf16[2,2,256,256]{3,2,0,1:T(8,128)(2,1)S(1)}, u32[]{:S(2)}, u32[]{:S(2)}) %collective-permute-start.22) | collective-permute-done | bytes 524320 | tf_op jit(solution)/shard_map/ppermute | solution.py:14
  349.8 3.0 collective-permute-start.23
  353.3 7.5 %collective-permute-done.17 = bf16[2,2,256,256]{3,2,1,0:T(8,128)(2,1)S(1)} collective-permute-done((bf16[2,2,256,256]{3,2,1,0:T(8,128)(2,1)S(1)}, bf16[2,2,256,256]{3,2,1,0:T(8,128)(2,1)S(1)}, u32[]{:S(2)}, u32[]{:S(2)}) %collective-permute-start.17) | collective-permute-done | bytes 524320 | tf_op jit(solution)/shard_map/ppermute | solution.py:14
  361.8 2.9 collective-permute-start.18
  365.8 3.8 collective-permute-done.23
  371.4 3.2 collective-permute-done.18
  (215 shorter events, 89.9 us)
Async XLA Ops:
  7.2 220.7 %all-reduce.2.cloned.1.call-start = ((), (), s32[]{:S(2)}) async-start(), calls=%async_computation | async-start | bytes 12582912 | tf_op jit(solution)/shard_map/psum | solution.py:166
  8.6 7.5 %collective-permute-start = (bf16[1,1,1,1,80,1024]{5,4,3,2,1,0:T(8,128)(2,1)S(1)}, bf16[1,1,1,1,80,1024]{5,4,3,2,1,0:T(8,128)(2,1)S(1)}, u32[]{:S(2)}, u32[]{:S(2)}) collective-permute-start(bf16[1,1,1,1,80,1024]{5,4,3,2,1,0:T(8,128)(2,1)S(1)} %get-tuple-element.50), channel_id=1, source_target_pairs={{0,4},{1,5},{2,6},{3,7},{4,0},{5,1},{6,2},{7,3},{8,12},{9,13},{10,... | collective-permute-start | bytes 491528 | tf_op jit(solution)/shard_map/ppermute | solution.py:14
  10.2 6.9 %collective-permute-start.1 = (bf16[1,1,1,1,80,1024]{5,4,3,2,1,0:T(8,128)(2,1)S(1)}, bf16[1,1,1,1,80,1024]{5,4,3,2,1,0:T(8,128)(2,1)S(1)}, u32[]{:S(2)}, u32[]{:S(2)}) collective-permute-start(bf16[1,1,1,1,80,1024]{5,4,3,2,1,0:T(8,128)(2,1)S(1)} %get-tuple-element.51), channel_id=1, source_target_pairs={{0,12},{1,13},{2,14},{3,15},{4,8},{5,9},{6,10},{7,11},{8,4},{9,5},... | collective-permute-start | bytes 491528 | tf_op jit(solution)/shard_map/ppermute | solution.py:14
  20.7 8.8 %collective-permute-start.4 = (bf16[1,1,1,2,80,1024]{5,4,3,2,1,0:T(8,128)(2,1)S(1)}, bf16[1,1,1,2,80,1024]{5,4,3,2,1,0:T(8,128)(2,1)S(1)}, u32[]{:S(2)}, u32[]{:S(2)}) collective-permute-start(bf16[1,1,1,2,80,1024]{5,4,3,2,1,0:T(8,128)(2,1)S(1)} %pad_maximum_fusion.20), channel_id=1, source_target_pairs={{0,12},{1,13},{2,14},{3,15},{4,8},{5,9},{6,10},{7,11},{8,4},{9,5},... | collective-permute-start | bytes 983048 | tf_op jit(solution)/shard_map/ppermute | solution.py:14
  21.9 7.5 %collective-permute-start.5 = (bf16[1,1,2,1,80,1024]{5,4,3,2,1,0:T(8,128)(2,1)S(1)}, bf16[1,1,2,1,80,1024]{5,4,3,2,1,0:T(8,128)(2,1)S(1)}, u32[]{:S(2)}, u32[]{:S(2)}) collective-permute-start(bf16[1,1,2,1,80,1024]{5,4,3,2,1,0:T(8,128)(2,1)S(1)} %pad_maximum_fusion.21), channel_id=1, source_target_pairs={{0,4},{1,5},{2,6},{3,7},{4,0},{5,1},{6,2},{7,3},{8,12},{9,13},{10,... | collective-permute-start | bytes 983048 | tf_op jit(solution)/shard_map/ppermute | solution.py:14
  21.9 8.4 %collective-permute-start.6 = (bf16[1,2,1,1,80,1024]{5,4,3,2,1,0:T(8,128)(2,1)S(1)}, bf16[1,2,1,1,80,1024]{5,4,3,2,1,0:T(8,128)(2,1)S(1)}, u32[]{:S(2)}, u32[]{:S(2)}) collective-permute-start(bf16[1,2,1,1,80,1024]{5,4,3,2,1,0:T(8,128)(2,1)S(1)} %pad_maximum_fusion.22), channel_id=1, source_target_pairs={{0,3},{1,2},{2,1},{3,0},{4,7},{5,6},{6,5},{7,4},{8,11},{9,10},{10,... | collective-permute-start | bytes 983048 | tf_op jit(solution)/shard_map/ppermute | solution.py:14
  24.1 7.2 %collective-permute-start.7 = (bf16[2,1,1,1,80,1024]{5,4,3,2,1,0:T(8,128)(2,1)S(1)}, bf16[2,1,1,1,80,1024]{5,4,3,2,1,0:T(8,128)(2,1)S(1)}, u32[]{:S(2)}, u32[]{:S(2)}) collective-permute-start(bf16[2,1,1,1,80,1024]{5,4,3,2,1,0:T(8,128)(2,1)S(1)} %pad_maximum_fusion.23), channel_id=1, source_target_pairs={{0,1},{1,0},{2,3},{3,2},{4,5},{5,4},{6,7},{7,6},{8,9},{9,8},{10,11... | collective-permute-start | bytes 983048 | tf_op jit(solution)/shard_map/ppermute | solution.py:14
  31.8 13.4 %collective-permute-start.10 = (bf16[2,2,1,1,80,1024]{5,4,3,2,1,0:T(8,128)(2,1)S(1)}, bf16[2,2,1,1,80,1024]{5,4,3,2,1,0:T(8,128)(2,1)S(1)}, u32[]{:S(2)}, u32[]{:S(2)}) collective-permute-start(bf16[2,2,1,1,80,1024]{5,4,3,2,1,0:T(8,128)(2,1)S(1)} %pad_maximum_fusion.18), channel_id=1, source_target_pairs={{0,4},{1,5},{2,6},{3,7},{4,0},{5,1},{6,2},{7,3},{8,12},{9,13},{10,... | collective-permute-start | bytes 1966088 | tf_op jit(solution)/shard_map/ppermute | solution.py:14
  33.8 14.0 %collective-permute-start.11 = (bf16[2,2,1,1,80,1024]{5,4,3,2,1,0:T(8,128)(2,1)S(1)}, bf16[2,2,1,1,80,1024]{5,4,3,2,1,0:T(8,128)(2,1)S(1)}, u32[]{:S(2)}, u32[]{:S(2)}) collective-permute-start(bf16[2,2,1,1,80,1024]{5,4,3,2,1,0:T(8,128)(2,1)S(1)} %pad_maximum_fusion.19), channel_id=1, source_target_pairs={{0,12},{1,13},{2,14},{3,15},{4,8},{5,9},{6,10},{7,11},{8,4},{9,5},... | collective-permute-start | bytes 1966088 | tf_op jit(solution)/shard_map/ppermute | solution.py:14
  35.9 12.2 %collective-permute-start.8 = (bf16[1,1,2,2,80,1024]{5,4,3,2,1,0:T(8,128)(2,1)S(1)}, bf16[1,1,2,2,80,1024]{5,4,3,2,1,0:T(8,128)(2,1)S(1)}, u32[]{:S(2)}, u32[]{:S(2)}) collective-permute-start(bf16[1,1,2,2,80,1024]{5,4,3,2,1,0:T(8,128)(2,1)S(1)} %pad_maximum_fusion.16), channel_id=1, source_target_pairs={{0,1},{1,0},{2,3},{3,2},{4,5},{5,4},{6,7},{7,6},{8,9},{9,8},{10,11... | collective-permute-start | bytes 1966088 | tf_op jit(solution)/shard_map/ppermute | solution.py:14
  35.9 13.9 %collective-permute-start.9 = (bf16[1,1,2,2,80,1024]{5,4,3,2,1,0:T(8,128)(2,1)S(1)}, bf16[1,1,2,2,80,1024]{5,4,3,2,1,0:T(8,128)(2,1)S(1)}, u32[]{:S(2)}, u32[]{:S(2)}) collective-permute-start(bf16[1,1,2,2,80,1024]{5,4,3,2,1,0:T(8,128)(2,1)S(1)} %pad_maximum_fusion.17), channel_id=1, source_target_pairs={{0,3},{1,2},{2,1},{3,0},{4,7},{5,6},{6,5},{7,4},{8,11},{9,10},{10,... | collective-permute-start | bytes 1966088 | tf_op jit(solution)/shard_map/ppermute | solution.py:14
  50.7 26.7 %collective-permute-start.12 = (bf16[1,2,2,2,80,1024]{5,4,3,2,1,0:T(8,128)(2,1)S(1)}, bf16[1,2,2,2,80,1024]{5,4,3,2,1,0:T(8,128)(2,1)S(1)}, u32[]{:S(2)}, u32[]{:S(2)}) collective-permute-start(bf16[1,2,2,2,80,1024]{5,4,3,2,1,0:T(8,128)(2,1)S(1)} %pad_maximum_fusion.4), channel_id=1, source_target_pairs={{0,3},{1,2},{2,1},{3,0},{4,7},{5,6},{6,5},{7,4},{8,11},{9,10},{10,... | collective-permute-start | bytes 3932168 | tf_op jit(solution)/shard_map/ppermute | solution.py:14
  52.0 25.4 %collective-permute-start.13 = (bf16[2,1,2,2,80,1024]{5,4,3,2,1,0:T(8,128)(2,1)S(1)}, bf16[2,1,2,2,80,1024]{5,4,3,2,1,0:T(8,128)(2,1)S(1)}, u32[]{:S(2)}, u32[]{:S(2)}) collective-permute-start(bf16[2,1,2,2,80,1024]{5,4,3,2,1,0:T(8,128)(2,1)S(1)} %pad_maximum_fusion.5), channel_id=1, source_target_pairs={{0,1},{1,0},{2,3},{3,2},{4,5},{5,4},{6,7},{7,6},{8,9},{9,8},{10,11... | collective-permute-start | bytes 3932168 | tf_op jit(solution)/shard_map/ppermute | solution.py:14
  53.4 24.4 %collective-permute-start.14 = (bf16[2,2,1,2,80,1024]{5,4,3,2,1,0:T(8,128)(2,1)S(1)}, bf16[2,2,1,2,80,1024]{5,4,3,2,1,0:T(8,128)(2,1)S(1)}, u32[]{:S(2)}, u32[]{:S(2)}) collective-permute-start(bf16[2,2,1,2,80,1024]{5,4,3,2,1,0:T(8,128)(2,1)S(1)} %pad_maximum_fusion.6), channel_id=1, source_target_pairs={{0,12},{1,13},{2,14},{3,15},{4,8},{5,9},{6,10},{7,11},{8,4},{9,5},... | collective-permute-start | bytes 3932168 | tf_op jit(solution)/shard_map/ppermute | solution.py:14
  54.7 24.1 %collective-permute-start.15 = (bf16[2,2,2,1,80,1024]{5,4,3,2,1,0:T(8,128)(2,1)S(1)}, bf16[2,2,2,1,80,1024]{5,4,3,2,1,0:T(8,128)(2,1)S(1)}, u32[]{:S(2)}, u32[]{:S(2)}) collective-permute-start(bf16[2,2,2,1,80,1024]{5,4,3,2,1,0:T(8,128)(2,1)S(1)} %pad_maximum_fusion.7), channel_id=1, source_target_pairs={{0,4},{1,5},{2,6},{3,7},{4,0},{5,1},{6,2},{7,3},{8,12},{9,13},{10,... | collective-permute-start | bytes 3932168 | tf_op jit(solution)/shard_map/ppermute | solution.py:14
  311.3 16.1 %collective-permute-start.21 = (bf16[2,4,512,256]{3,2,1,0:T(8,128)(2,1)}, bf16[2,4,512,256]{3,2,1,0:T(8,128)(2,1)}, u32[]{:S(2)}, u32[]{:S(2)}) collective-permute-start(bf16[2,4,512,256]{3,2,1,0:T(8,128)(2,1)} %select_bitcast_fusion), channel_id=1, source_target_pairs={{0,16},{16,0},{32,48},{48,32},{64,80},{80,64},{96,112},{112,96},{1... | collective-permute-start | bytes 6291464 | tf_op jit(solution)/shard_map/ppermute | solution.py:14
  334.8 14.8 %collective-permute-start.22 = (bf16[2,2,256,256]{3,2,0,1:T(8,128)(2,1)S(1)}, bf16[2,2,256,256]{3,2,0,1:T(8,128)(2,1)S(1)}, u32[]{:S(2)}, u32[]{:S(2)}) collective-permute-start(bf16[2,2,256,256]{3,2,0,1:T(8,128)(2,1)S(1)} %select_bitcast_fusion.3), channel_id=1, source_target_pairs={{0,32},{16,48},{32,0},{48,16},{64,96},{80,112},{96,64},{112,80},{1... | collective-permute-start | bytes 1572872 | tf_op jit(solution)/shard_map/ppermute | solution.py:14
  336.7 16.2 %collective-permute-start.24 = (bf16[2,2,256,256]{3,2,0,1:T(8,128)(2,1)S(1)}, bf16[2,2,256,256]{3,2,0,1:T(8,128)(2,1)S(1)}, u32[]{:S(2)}, u32[]{:S(2)}) collective-permute-start(bf16[2,2,256,256]{3,2,0,1:T(8,128)(2,1)S(1)} %select_bitcast_fusion.2), channel_id=1, source_target_pairs={{0,96},{16,112},{32,64},{48,80},{64,32},{80,48},{96,0},{112,16},{1... | collective-permute-start | bytes 1572872 | tf_op jit(solution)/shard_map/ppermute | solution.py:14
  339.2 21.7 %collective-permute-start.17 = (bf16[2,2,256,256]{3,2,1,0:T(8,128)(2,1)S(1)}, bf16[2,2,256,256]{3,2,1,0:T(8,128)(2,1)S(1)}, u32[]{:S(2)}, u32[]{:S(2)}) collective-permute-start(bf16[2,2,256,256]{3,2,1,0:T(8,128)(2,1)S(1)} %get-tuple-element.137), channel_id=1, source_target_pairs={{0,32},{16,48},{32,0},{48,16},{64,96},{80,112},{96,64},{112,80},{1... | collective-permute-start | bytes 1572872 | tf_op jit(solution)/shard_map/ppermute | solution.py:14
  340.1 24.5 %collective-permute-start.19 = (bf16[2,2,256,256]{3,2,0,1:T(8,128)(2,1)S(1)}, bf16[2,2,256,256]{3,2,0,1:T(8,128)(2,1)S(1)}, u32[]{:S(2)}, u32[]{:S(2)}) collective-permute-start(bf16[2,2,256,256]{3,2,0,1:T(8,128)(2,1)S(1)} %select_bitcast_fusion.4), channel_id=1, source_target_pairs={{0,96},{16,112},{32,64},{48,80},{64,32},{80,48},{96,0},{112,16},{1... | collective-permute-start | bytes 1572872 | tf_op jit(solution)/shard_map/ppermute | solution.py:14
  349.8 19.7 %collective-permute-start.23 = (bf16[2,256,256]{2,1,0:T(8,128)(2,1)S(1)}, bf16[2,256,256]{2,1,0:T(8,128)(2,1)S(1)}, u32[]{:S(2)}, u32[]{:S(2)}) collective-permute-start(bf16[2,256,256]{2,1,0:T(8,128)(2,1)S(1)} %select_bitcast_fusion.7), channel_id=1, source_target_pairs={{0,96},{16,112},{32,64},{48,80},{64,32},{80,48},{96,0},{112,16},{1... | collective-permute-start | bytes 786440 | tf_op jit(solution)/shard_map/ppermute | solution.py:14
  353.1 16.6 %collective-permute-start.25 = (bf16[2,256,256]{2,1,0:T(8,128)(2,1)S(1)}, bf16[2,256,256]{2,1,0:T(8,128)(2,1)S(1)}, u32[]{:S(2)}, u32[]{:S(2)}) collective-permute-start(bf16[2,256,256]{2,1,0:T(8,128)(2,1)S(1)} %select_bitcast_fusion.6), channel_id=1, source_target_pairs={{0,32},{16,48},{32,0},{48,16},{64,96},{80,112},{96,64},{112,80},{1... | collective-permute-start | bytes 786440 | tf_op jit(solution)/shard_map/ppermute | solution.py:14
  361.8 12.8 %collective-permute-start.18 = (bf16[2,256,256]{2,1,0:T(8,128)(2,1)}, bf16[2,256,256]{2,1,0:T(8,128)(2,1)}, u32[]{:S(2)}, u32[]{:S(2)}) collective-permute-start(bf16[2,256,256]{2,1,0:T(8,128)(2,1)} %fusion.55), channel_id=1, source_target_pairs={{0,96},{16,112},{32,64},{48,80},{64,32},{80,48},{96,0},{112,16},{1... | collective-permute-start | bytes 786440 | tf_op jit(solution)/shard_map/ppermute | solution.py:14
  365.6 10.0 %collective-permute-start.20 = (bf16[2,256,256]{2,1,0:T(8,128)(2,1)}, bf16[2,256,256]{2,1,0:T(8,128)(2,1)}, u32[]{:S(2)}, u32[]{:S(2)}) collective-permute-start(bf16[2,256,256]{2,1,0:T(8,128)(2,1)} %select_bitcast_fusion.8), channel_id=1, source_target_pairs={{0,32},{16,48},{32,0},{48,16},{64,96},{80,112},{96,64},{112,80},{1... | collective-permute-start | bytes 786440 | tf_op jit(solution)/shard_map/ppermute | solution.py:14
  (44 other events, 275.3 us)
Sparse Core Ops, SparseCore 0:
  105.5 122.3 all-reduce.1
